TPU v7x, 512 devices: a whole 4x8x8 slice. The times are simulated.
512 devices in a mesh: cam: 16 (over x_lo, y), space: 32 (over x_hi, z, core).
Axes of the slice: x: 4 (x_hi: 2, x_lo: 2; x = x_hi * 2 + x_lo), y: 8, z: 8, core: 2. Of those that a mesh axis runs over, the one named last changes fastest.
Arguments:
- features: float32 [64, 131072], P(None, ('cam', 'space')), may hold values from -6 to 6
- positions: float32 [3, 131072], P(None, ('cam', 'space')), may hold values from -6144 to 6144, as said below
- spreads: float32 [131072], P(('cam', 'space')), may hold values from 16 to 64
- logits: float32 [131072], P(('cam', 'space')), may hold values from -6 to -2
- camera: float32 [16, 3], replicated, may hold values from -1 to 1
- decoder: bfloat16 [64, 512], replicated, may hold values from -0.75 to 0.75
- tile_lists: int32 [16, 32, 16, 256], P('cam', 'space'), may hold values from 0 to 8191, as said below
- counts: int32 [16, 32, 16], P('cam', 'space'), may hold values from 1 to 256, as said below
- targets: bfloat16 [16, 32, 16, 256, 512], P('cam', 'space'), may hold values from -6 to 6
Outputs:
- grad_features: float32 [64, 131072], P(None, ('cam', 'space'))
- grad_logits: float32 [131072], P(('cam', 'space'))
Inputs may be any that keep to these rules, and one draw needn't show every extreme that they name: `positions`: rows are x, y and depth; depth lies between 4 and 8. `tile_lists`: the list of tile (c, s, j) names only ids j * 256 + q or 4096 + j * 256 + q with 0 <= q < 256, no id twice; lists of tile row 0 name only ids below 4096. `counts`: some tile has all 256 entries live.
All inputs are finite; a program needn't handle non-finite values.
Results may differ from a plain program's by a relative error of at most 0.003.
Values may be sent and summed in bfloat16 or wider, within the bound.
No kernel may reach another device: no remote copies, remote signals or barrier semaphores. Data moves between devices by JAX's collectives and lax.ppermute only.
A program may use at most 64 MiB of HBM per device.

v0:
```python
import jax
import jax.numpy as jnp
from jax import lax
from jax.sharding import PartitionSpec as P

TS = 16


def shifted(shard, axis, by):
    length = lax.axis_size(axis)
    pairs = [(i, i + by) for i in range(length) if 0 <= i + by < length]
    return lax.ppermute(shard, axis, pairs)


def project_terms(
    gathered, viewers, tile_row, columns, live_counts, grad_maker, image_width, image_height
):
    channels = gathered.shape[0] - 5
    tiles_here = gathered.shape[1]
    length = gathered.shape[2]
    step_len = 128
    block_count = length // step_len
    pixel_count = TS * TS
    feature_bf = gathered[:channels].astype(jnp.bfloat16)
    distance = gathered[channels + 2] - 0.05 * viewers[:, 2:3]
    centre_u = (gathered[channels] - 0.75 * TS * viewers[:, 0:1]) / distance + 0.5 * image_width
    centre_v = (
        gathered[channels + 1] - 0.75 * TS * viewers[:, 1:2]
    ) / distance + 0.5 * image_height
    radius = gathered[channels + 3] / distance
    sigmoid_open = jax.nn.sigmoid(gathered[channels + 4])
    opacity = 0.99 * sigmoid_open
    sigmoid_slope = 0.99 * sigmoid_open * (1.0 - sigmoid_open)
    pixel_id = jnp.arange(pixel_count, dtype=jnp.int32)
    pixel_u = (columns[:, None] * TS + pixel_id[None, :] % TS).astype(jnp.float32) + 0.5
    pixel_v = (tile_row * TS + pixel_id // TS).astype(jnp.float32) + 0.5
    alive_mask = (jnp.arange(length, dtype=jnp.int32)[None, :] < live_counts[:, None]).astype(
        jnp.float32
    )
    logit_gate_all = alive_mask * sigmoid_slope
    steps_used = (jnp.max(live_counts) + step_len - 1) // step_len

    def block_terms(first_entry):

        def window_of(source_array):
            return lax.dynamic_slice_in_dim(
                source_array, first_entry, step_len, axis=source_array.ndim - 1
            )

        delta_u = pixel_u[:, :, None] - window_of(centre_u)[:, None, :]
        delta_v = pixel_v[None, :, None] - window_of(centre_v)[:, None, :]
        spread = window_of(radius)[:, None, :]
        falloff = jnp.exp(-(delta_u * delta_u + delta_v * delta_v) / (2.0 * spread * spread))
        opaque = (window_of(opacity) * window_of(alive_mask))[:, None, :] * falloff
        log_keep = jnp.log(1.0 - opaque)
        inner_log = jnp.cumsum(log_keep, axis=2) - log_keep
        return (
            falloff,
            opaque,
            log_keep,
            inner_log,
            window_of(feature_bf),
            window_of(logit_gate_all),
        )

    def forward(position, state_in):
        log_start, feature_sum, starts = state_in
        first_entry = position * step_len
        falloff, opaque, log_keep, inner_log, block_feat, unused = block_terms(first_entry)
        weight = opaque * jnp.exp(log_start[:, :, None] + inner_log)
        feature_sum = feature_sum + jnp.einsum(
            "tpk,ctk->tcp",
            weight.astype(jnp.bfloat16),
            block_feat,
            preferred_element_type=jnp.float32,
        )
        starts = lax.dynamic_update_index_in_dim(starts, log_start, position, 0)
        return (log_start + jnp.sum(log_keep, axis=2), feature_sum, starts)

    initial = (
        jnp.zeros((tiles_here, pixel_count), jnp.float32),
        jnp.zeros((tiles_here, channels, pixel_count), jnp.float32),
        jnp.zeros((block_count, tiles_here, pixel_count), jnp.float32),
    )
    unused_log, feature_sum, starts = lax.fori_loop(0, steps_used, forward, initial)
    composite = feature_sum.astype(jnp.bfloat16)
    pixel_grad = grad_maker(composite).astype(jnp.bfloat16)

    def backward(reverse_turn, state_in):
        behind_sum, feature_grad, logit_grad = state_in
        position = steps_used - 1 - reverse_turn
        first_entry = position * step_len
        falloff, opaque, log_keep, inner_log, block_feat, logit_gate = block_terms(first_entry)
        keep_to = jnp.exp(
            lax.dynamic_index_in_dim(starts, position, 0, keepdims=False)[:, :, None] + inner_log
        )
        weight = opaque * keep_to
        weight_bf = weight.astype(jnp.bfloat16)
        contrib = jnp.einsum(
            "tcp,ctk->tpk", pixel_grad, block_feat, preferred_element_type=jnp.float32
        )
        weighted = weight * contrib
        block_total = jnp.sum(weighted, axis=2)
        behind = behind_sum[:, :, None] + block_total[:, :, None] - jnp.cumsum(weighted, axis=2)
        dopaque = keep_to * contrib - behind / (1.0 - opaque)
        logit_part = logit_gate * jnp.sum(dopaque * falloff, axis=1)
        feature_part = jnp.einsum(
            "tpk,tcp->ctk", weight_bf, pixel_grad, preferred_element_type=jnp.float32
        )
        feature_grad = lax.dynamic_update_slice_in_dim(
            feature_grad, feature_part, first_entry, axis=2
        )
        logit_grad = lax.dynamic_update_slice_in_dim(logit_grad, logit_part, first_entry, axis=1)
        return (behind_sum + block_total, feature_grad, logit_grad)

    initial_back = (
        jnp.zeros((tiles_here, pixel_count), jnp.float32),
        jnp.zeros((channels, tiles_here, length), jnp.float32),
        jnp.zeros((tiles_here, length), jnp.float32),
    )
    unused_behind, feature_grad, logit_grad = lax.fori_loop(0, steps_used, backward, initial_back)
    return (feature_grad, logit_grad)


def full_target_rule(pixel_targets, decoder):
    decoder_wide = decoder.astype(jnp.float32)

    def make_grad(composite):
        decoded = jnp.einsum("tcp,cd->tpd", composite, decoder, preferred_element_type=jnp.float32)
        residual = decoded - pixel_targets.astype(jnp.float32)
        return jnp.einsum("tpd,cd->tcp", residual, decoder_wide, precision=lax.Precision.HIGHEST)

    return make_grad


def on_device(features, positions, spreads, logits, camera, decoder, tile_lists, counts, targets):
    channels = features.shape[0]
    length = features.shape[1]
    camera_count = lax.axis_size("cam")
    space_count = lax.axis_size("space")
    camera_id = lax.axis_index("cam")
    tile_row = lax.axis_index("space")
    image_width = TS * camera_count
    image_height = TS * space_count
    block_rows = camera_count * length
    own_slab = jnp.concatenate([features, positions, spreads[None], logits[None]], axis=0)
    upper_slab = shifted(own_slab, "space", 1)
    both_slabs = lax.all_gather(jnp.stack([own_slab, upper_slab]), "cam", axis=2, tiled=True)
    gauss_table = jnp.concatenate([both_slabs[0], both_slabs[1]], axis=1)
    entries = tile_lists[0, 0]
    picker = (jnp.arange(camera_count, dtype=jnp.int32) == camera_id).astype(jnp.float32)
    viewers = jnp.broadcast_to(jnp.sum(camera * picker[:, None], axis=0), (camera_count, 3))
    columns = jnp.arange(camera_count, dtype=jnp.int32)
    gathered = jnp.take(gauss_table, entries, axis=1)
    grad_maker = full_target_rule(targets[0, 0], decoder)
    feature_grad, logit_grad = project_terms(
        gathered, viewers, tile_row, columns, counts[0, 0], grad_maker, image_width, image_height
    )
    values = jnp.concatenate([feature_grad, logit_grad[None]], axis=0)
    totals = jnp.zeros((channels + 1, 2 * block_rows), jnp.float32).at[:, entries].add(values)
    returned = shifted(totals[:, block_rows:], "space", -1)
    summed = lax.psum_scatter(
        totals[:, :block_rows] + returned, "cam", scatter_dimension=1, tiled=True
    )
    return (summed[:channels], summed[channels])


def solution(mesh):
    placed = (
        P(None, ("cam", "space")),
        P(None, ("cam", "space")),
        P(("cam", "space")),
        P(("cam", "space")),
        P(),
        P(),
        P("cam", "space", None, None),
        P("cam", "space", None),
        P("cam", "space", None, None, None),
    )
    return jax.shard_map(
        on_device,
        mesh=mesh,
        in_specs=placed,
        out_specs=(P(None, ("cam", "space")), P(("cam", "space"))),
        check_vma=False,
    )
```

profile of v0, /device:TPU:4, one launch (start us, length us, event | category | flops | bytes accessed | tf_op | source)
XLA Modules:
  0.0 300.1 jit_solution(15788181093214662596)
XLA Ops:
  10.8 1.9 collective-permute-start
  12.9 10.9 %collective-permute-done = f32[69,256]{0,1:T(8,128)S(1)} collective-permute-done((f32[69,256]{0,1:T(8,128)S(1)}, f32[69,256]{0,1:T(8,128)S(1)}, u32[]{:S(2)}, u32[]{:S(2)}) %collective-permute-start) | collective-permute-done | bytes 70688 | tf_op jit(solution)/shard_map/ppermute | solution.py:12
  28.9 72.8 %all-gather.2.cloned.1.call-done = f32[2,69,4096]{1,2,0:T(8,128)} async-done(((f32[2,69,256]{1,2,0:T(8,128)}), f32[2,69,4096]{1,2,0:T(8,128)}) %all-gather.2.cloned.1.call-update) | async-done | bytes 2261008 | tf_op jit(solution)/shard_map/all_gather | solution.py:148
  101.7 2.5 slice_bitcast_fusion.1
  104.2 2.2 pad_maximum_fusion
  106.4 13.0 %gather_fusion = f32[4096,69]{1,0:T(8,128)S(1)} fusion(f32[69,8192]{0,1:T(8,128)} %pad_maximum_fusion, s32[4096]{0:T(1024)S(1)} %broadcast_clamp_fusion), kind=kCustom, calls=%fused_computation | custom fusion | bytes 2277376 | tf_op jit(solution)/shard_map/jit(_take)/gather | solution.py:154
  121.0 11.3 %while.32 = (s32[]{:T(128)}, f32[16,256]{1,0:T(8,128)S(1)}, f32[16,64,256]{2,1,0:T(8,128)S(1)}, f32[2,16,256]{2,1,0:T(8,128)S(1)}, s32[]{:T(128)}, /*index=5*/f3...) while((s32[]{:T(128)}, f32[16,256]{1,0:T(8,128)S(1)}, ...), condition=%wide.region_5.6_spmd.clone, body=%wide.region_2.5_spmd.clone.sunk | while | flops 150754048 | bytes 4895069 | solution.py:85
  123.1 2.8 multiply_convert_fusion.2
  128.7 2.8 multiply_convert_fusion.2
  134.4 4.9 %fusion.43 = bf16[16,64,256]{2,1,0:T(8,128)(2,1)S(1)} fusion(f32[16,256,512]{2,1,0:T(8,128)S(1)} %fusion.44, bf16[1,1,16,256,512]{4,3,2,1,0:T(8,128)(2,1)S(1)} %copy-done.1, bf16[64,512]{1,0:T(8,128)(2,1)S(1)} %copy-done), kind=kOutput, calls=%fused_computation.78 | convolution fusion | flops 1615069184 | bytes 13172736 | tf_op jit(solution)/shard_map/tpd,cd->tcp/dot_general | solution.py:131
  139.4 25.9 %while.33 = (s32[]{:T(128)}, f32[16,256]{1,0:T(8,128)S(1)}, f32[64,16,256]{2,0,1:T(8,128)S(1)}, f32[16,256]{1,0:T(8,128)S(1)}, s32[]{:T(128)}, /*index=5*/s32[]{...) while((s32[]{:T(128)}, f32[16,256]{1,0:T(8,128)S(1)}, ...), condition=%wide.region_11.12_spmd.clone, body=%wide.region_6.11_spmd.clone.sunk | while | flops 295195392 | bytes 27490700 | solution.py:121
  142.3 2.2 fusion.93
  144.5 2.5 fusion.92
  148.2 4.2 %fusion.95 = f32[16,128]{1,0:T(8,128)S(1)} fusion(f32[16,128,256]{2,1,0:T(8,128)S(1)} %get-tuple-element.746, f32[16,256,128]{1,0,2:T(8,128)S(1)} %fusion.94, f32[16,256]{1,0:T(8,128)S(1)} %add.491, f32[16,128]{1,0:T(8,128)S(1)} %get-tuple-element.741, f32[16,128]{1,0:T(8,128)S(1)} %get-tuple-element.742, f32[256]{0:T(256)S(1)} %fusion.90, ...), kind=kLoop, calls=%fused_computation.35.clone.1 | loop fusion | flops 8910848 | bytes 6382592 | tf_op jit(solution)/shard_map/while/body/reduce_sum | solution.py:106
  155.1 2.2 fusion.93
  157.3 2.5 fusion.92
  161.1 4.2 %fusion.95 = f32[16,128]{1,0:T(8,128)S(1)} fusion(f32[16,128,256]{2,1,0:T(8,128)S(1)} %get-tuple-element.746, f32[16,256,128]{1,0,2:T(8,128)S(1)} %fusion.94, f32[16,256]{1,0:T(8,128)S(1)} %add.491, f32[16,128]{1,0:T(8,128)S(1)} %get-tuple-element.741, f32[16,128]{1,0:T(8,128)S(1)} %get-tuple-element.742, f32[256]{0:T(256)S(1)} %fusion.90, ...), kind=kLoop, calls=%fused_computation.35.clone.1 | loop fusion | flops 8910848 | bytes 6382592 | tf_op jit(solution)/shard_map/while/body/reduce_sum | solution.py:106
  166.3 24.5 %scatter_custom_fusion = f32[65,8192]{0,1:T(8,128)} fusion(s32[4096]{0:T(1024)S(1)} %bitcast.99, f32[4096,65]{1,0:T(8,128)S(1)} %bitcast.95, f32[]{:T(128)} %constant.142.clone.1), kind=kCustom, calls=%fused_computation.75 | custom fusion | flops 266240 | bytes 2129924 | tf_op jit(solution)/shard_map/scatter-add | solution.py:160
  193.3 1.9 collective-permute-start.1
  195.2 13.7 %collective-permute-done.1 = f32[65,4096]{1,0:T(8,128)} collective-permute-done((f32[65,4096]{1,0:T(8,128)S(1)}, f32[65,4096]{1,0:T(8,128)}, u32[]{:S(2)}, u32[]{:S(2)}) %collective-permute-start.1) | collective-permute-done | bytes 1064992 | tf_op jit(solution)/shard_map/ppermute | solution.py:12
  208.9 1.8 copy.73
  210.7 3.1 %slice_add_fusion = f32[65,4096]{0,1:T(8,128)} fusion(f32[65,4096]{0,1:T(8,128)S(1)} %copy.73, f32[65,8192]{0,1:T(8,128)} %scatter_custom_fusion), kind=kLoop, calls=%fused_computation.72 | loop fusion | flops 266240 | bytes 3194880 | tf_op jit(solution)/shard_map/add | solution.py:163
  213.9 76.1 %reduce-scatter.2.cloned.1.call-done = f32[65,256]{0,1:T(8,128)} async-done(((f32[65,4096]{0,1:T(8,128)}), f32[65,256]{0,1:T(8,128)}) %reduce-scatter.2.cloned.1.call-update) | async-done | bytes 66576 | tf_op jit(solution)/shard_map/reduce_scatter | solution.py:162
  291.6 1.7 slice_reduce_fusion
  (104 shorter events, 27.9 us)
Async XLA Ops:
  7.2 125.1 %copy-start = (bf16[64,512]{1,0:T(8,128)(2,1)S(1)}, bf16[64,512]{1,0:T(8,128)(2,1)}, u32[]{:S(2)}) copy-start(bf16[64,512]{1,0:T(8,128)(2,1)} %param.18) | copy-start | bytes 196612
  7.2 17.4 %copy-start.3 = (s32[1,1,16]{2,1,0:T(1,128)S(1)}, s32[1,1,16]{2,1,0:T(1,128)}, u32[]{:S(2)}) copy-start(s32[1,1,16]{2,1,0:T(1,128)} %param.20) | copy-start | bytes 196
  7.2 18.7 %copy-start.4 = (f32[16,3]{0,1:T(4,128)S(1)}, f32[16,3]{0,1:T(4,128)}, u32[]{:S(2)}) copy-start(f32[16,3]{0,1:T(4,128)} %param.17) | copy-start | bytes 580
  7.2 20.9 %copy-start.2 = (s32[1,1,16,256]{3,2,1,0:T(8,128)S(1)}, s32[1,1,16,256]{3,2,1,0:T(8,128)}, u32[]{:S(2)}) copy-start(s32[1,1,16,256]{3,2,1,0:T(8,128)} %param.19) | copy-start | bytes 49156
  7.2 94.5 %all-gather.2.cloned.1.call-start = ((), (), s32[]{:S(2)}) async-start(), calls=%async_computation.1 | async-start | bytes 4456448 | tf_op jit(solution)/shard_map/all_gather | solution.py:148
  10.8 13.0 %collective-permute-start = (f32[69,256]{0,1:T(8,128)S(1)}, f32[69,256]{0,1:T(8,128)S(1)}, u32[]{:S(2)}, u32[]{:S(2)}) collective-permute-start(f32[69,256]{0,1:T(8,128)S(1)} %pad_maximum_fusion.2), channel_id=1, source_target_pairs={{0,1},{1,2},{2,3},{3,4},{4,5},{5,6},{6,7},{7,8},{8,9},{9,10},{10,1... | collective-permute-start | bytes 211976 | tf_op jit(solution)/shard_map/ppermute | solution.py:12
  24.5 265.5 %reduce-scatter.2.cloned.1.call-start = ((), (), s32[]{:S(2)}) async-start(), calls=%async_computation.2 | async-start | bytes 2228224 | tf_op jit(solution)/shard_map/reduce_scatter | solution.py:162
  132.2 2.2 copy-start.1
  190.8 1.6 slice-start
  193.3 15.6 %collective-permute-start.1 = (f32[65,4096]{1,0:T(8,128)S(1)}, f32[65,4096]{1,0:T(8,128)}, u32[]{:S(2)}, u32[]{:S(2)}) collective-permute-start(f32[65,4096]{1,0:T(8,128)S(1)} %copy.72), channel_id=1, source_target_pairs={{1,0},{2,1},{3,2},{4,3},{5,4},{6,5},{7,6},{8,7},{9,8},{10,9},{11,1... | collective-permute-start | bytes 3194888 | tf_op jit(solution)/shard_map/ppermute | solution.py:12
Sparse Core Ops, SparseCore 0:
  24.7 76.9 all-gather.1
  214.0 75.9 reduce-scatter.1
where the time goes:
time: 301 us; the launch traced here: 300 us
  waiting for transfers between devices  174 us (58%)
  other arithmetic  56.9 us (19%)
  local copies, waits for them, and re-layouts  31.3 us (10%)
  between operations  17.1 us (6%)
  matrix products  16.6 us (6%)
  starting transfers between devices  3.92 us (1%)
    reduce_scatter x1, waiting for transfers between devices, on_device(): lax.psum_scatter(totals[:, :block_rows] + returned, 'cam', scatter_dimens...  76.1 us
    all_gather x1, waiting for transfers between devices, on_device(): lax.all_gather(jnp.stack([own_slab, upper_slab]), 'cam', axis=2, tiled=True)  72.8 us
    ppermute x2, waiting for transfers between devices, shifted(): return lax.ppermute(shard, axis, pairs)  24.6 us
    scatter-add x1, other arithmetic, on_device(): jnp.zeros((channels + 1, 2 * block_rows), jnp.float32).at[:, entries]  24.5 us
    gather x2, local copies, waits for them, and re-layouts, on_device(): gathered = jnp.take(gauss_table, entries, axis=1)  14 us
    reduce_sum x2, other arithmetic, backward(): logit_part = logit_gate * jnp.sum(dopaque * falloff, axis=1)  8.48 us
    another operation x4, other arithmetic, block_terms(): inner_log = jnp.cumsum(log_keep, axis=2) - log_keep  8.17 us
  transfers between devices with their start and end apart: 4, of which 4 were waited for; matrix products, arithmetic and copies ran while one was open for 1% of the time, Pallas kernels for 0%

commit v1 on v0

--- a/solution.py
+++ b/solution.py
@@ -145,7 +145,8 @@
     block_rows = camera_count * length
     own_slab = jnp.concatenate([features, positions, spreads[None], logits[None]], axis=0)
     upper_slab = shifted(own_slab, "space", 1)
-    both_slabs = lax.all_gather(jnp.stack([own_slab, upper_slab]), "cam", axis=2, tiled=True)
+    piece_in = jnp.stack([own_slab, upper_slab])
+    both_slabs = jnp.concatenate(lax.all_gather(piece_in, "cam"), 2)
     gauss_table = jnp.concatenate([both_slabs[0], both_slabs[1]], axis=1)
     entries = tile_lists[0, 0]
     picker = (jnp.arange(camera_count, dtype=jnp.int32) == camera_id).astype(jnp.float32)

time: 301 us -> 298 us (0.990)
  waiting for transfers between devices: 174 us -> 165 us
  other arithmetic: 56.9 us -> 60.9 us
    all_gather x1, waiting for transfers between devices: 72.8 us -> 65.6 us  [on_device(): both_slabs = jnp.concatenate(lax.all_gather(piece_in, 'cam'), 2)]
    all_gather x0 -> x1, local copies, waits for them, and re-layouts: none -> 4.7 us  [on_device(): both_slabs = jnp.concatenate(lax.all_gather(piece_in, 'cam'), 2)]
  transfers between devices with their start and end apart: 4 -> 4, of which waited for: 4 -> 4; matrix products, arithmetic and copies ran while one was open for 1% -> 2% of each run, Pallas kernels for 0% -> 0%
where the time goes in v1:
time: 298 us; the launch traced here: 297 us
  waiting for transfers between devices  165 us (55%)
  other arithmetic  60.9 us (20%)
  local copies, waits for them, and re-layouts  32.8 us (11%)
  between operations  16.9 us (6%)
  matrix products  16.6 us (6%)
  starting transfers between devices  3.92 us (1%)
    reduce_scatter x1, waiting for transfers between devices, on_device(): lax.psum_scatter(totals[:, :block_rows] + returned, 'cam', scatter_dimens...  75.5 us
    all_gather x1, waiting for transfers between devices, on_device(): both_slabs = jnp.concatenate(lax.all_gather(piece_in, 'cam'), 2)  65.6 us
    scatter-add x1, other arithmetic, on_device(): jnp.zeros((channels + 1, 2 * block_rows), jnp.float32).at[:, entries]  24.5 us
    ppermute x2, waiting for transfers between devices, shifted(): return lax.ppermute(shard, axis, pairs)  24.1 us
    gather x2, local copies, waits for them, and re-layouts, on_device(): gathered = jnp.take(gauss_table, entries, axis=1)  14 us
    reduce_sum x2, other arithmetic, backward(): logit_part = logit_gate * jnp.sum(dopaque * falloff, axis=1)  8.48 us
    another operation x4, other arithmetic, block_terms(): inner_log = jnp.cumsum(log_keep, axis=2) - log_keep  8.17 us
  transfers between devices with their start and end apart: 4, of which 4 were waited for; matrix products, arithmetic and copies ran while one was open for 2% of the time, Pallas kernels for 0%

profile of v1, /device:TPU:4, one launch (start us, length us, event | category | flops | bytes accessed | tf_op | source)
XLA Modules:
  0.0 297.1 jit_solution(16496471256614473071)
XLA Ops:
  8.1 1.9 collective-permute-start
  10.1 10.4 %collective-permute-done = f32[69,256]{1,0:T(8,128)S(1)} collective-permute-done((f32[69,256]{1,0:T(8,128)S(1)}, f32[69,256]{1,0:T(8,128)S(1)}, u32[]{:S(2)}, u32[]{:S(2)}) %collective-permute-start) | collective-permute-done | bytes 70688 | tf_op jit(solution)/shard_map/ppermute | solution.py:12
  28.8 65.6 %all-gather.3.cloned.1.call-done = f32[32,69,256]{2,1,0:T(8,128)} async-done(((f32[2,69,256]{2,1,0:T(8,128)}), f32[32,69,256]{2,1,0:T(8,128)}) %all-gather.3.cloned.1.call-update) | async-done | bytes 2261008 | tf_op jit(solution)/shard_map/all_gather | solution.py:149
  94.4 4.7 %copy.53 = f32[16,2,69,256]{2,3,0,1:T(8,128)} copy(f32[16,2,69,256]{3,2,1,0:T(8,128)} %bitcast.98) | data formatting | bytes 4521984 | tf_op jit(solution)/shard_map/all_gather | solution.py:149
  99.1 2.6 fusion.63
  101.8 2.2 pad_maximum_fusion
  104.0 13.0 %gather_fusion = f32[4096,69]{1,0:T(8,128)S(1)} fusion(f32[69,8192]{0,1:T(8,128)} %pad_maximum_fusion, s32[4096]{0:T(1024)S(1)} %broadcast_clamp_fusion), kind=kCustom, calls=%fused_computation | custom fusion | bytes 2277376 | tf_op jit(solution)/shard_map/jit(_take)/gather | solution.py:155
  118.6 11.3 %while.32 = (s32[]{:T(128)}, f32[16,256]{1,0:T(8,128)S(1)}, f32[16,64,256]{2,1,0:T(8,128)S(1)}, f32[2,16,256]{2,1,0:T(8,128)S(1)}, s32[]{:T(128)}, /*index=5*/f3...) while((s32[]{:T(128)}, f32[16,256]{1,0:T(8,128)S(1)}, ...), condition=%wide.region_5.6_spmd.clone, body=%wide.region_2.5_spmd.clone.sunk | while | flops 150754048 | bytes 4895069 | solution.py:85
  120.7 2.8 multiply_convert_fusion.2
  126.3 2.8 multiply_convert_fusion.2
  132.1 4.9 %fusion.43 = bf16[16,64,256]{2,1,0:T(8,128)(2,1)S(1)} fusion(f32[16,256,512]{2,1,0:T(8,128)S(1)} %fusion.44, bf16[1,1,16,256,512]{4,3,2,1,0:T(8,128)(2,1)S(1)} %copy-done.1, bf16[64,512]{1,0:T(8,128)(2,1)S(1)} %copy-done), kind=kOutput, calls=%fused_computation.76 | convolution fusion | flops 1615069184 | bytes 13172736 | tf_op jit(solution)/shard_map/tpd,cd->tcp/dot_general | solution.py:131
  137.1 25.9 %while.33 = (s32[]{:T(128)}, f32[16,256]{1,0:T(8,128)S(1)}, f32[64,16,256]{2,0,1:T(8,128)S(1)}, f32[16,256]{1,0:T(8,128)S(1)}, s32[]{:T(128)}, /*index=5*/s32[]{...) while((s32[]{:T(128)}, f32[16,256]{1,0:T(8,128)S(1)}, ...), condition=%wide.region_11.12_spmd.clone, body=%wide.region_6.11_spmd.clone.sunk | while | flops 295195392 | bytes 27490700 | solution.py:121
  139.9 2.2 fusion.94
  142.1 2.5 fusion.93
  145.8 4.2 %fusion.96 = f32[16,128]{1,0:T(8,128)S(1)} fusion(f32[16,128,256]{2,1,0:T(8,128)S(1)} %get-tuple-element.748, f32[16,256,128]{1,0,2:T(8,128)S(1)} %fusion.95, f32[16,256]{1,0:T(8,128)S(1)} %add.491, f32[16,128]{1,0:T(8,128)S(1)} %get-tuple-element.743, f32[16,128]{1,0:T(8,128)S(1)} %get-tuple-element.744, f32[256]{0:T(256)S(1)} %fusion.91, ...), kind=kLoop, calls=%fused_computation.35.clone.1 | loop fusion | flops 8910848 | bytes 6382592 | tf_op jit(solution)/shard_map/while/body/reduce_sum | solution.py:106
  152.7 2.2 fusion.94
  154.9 2.5 fusion.93
  158.7 4.2 %fusion.96 = f32[16,128]{1,0:T(8,128)S(1)} fusion(f32[16,128,256]{2,1,0:T(8,128)S(1)} %get-tuple-element.748, f32[16,256,128]{1,0,2:T(8,128)S(1)} %fusion.95, f32[16,256]{1,0:T(8,128)S(1)} %add.491, f32[16,128]{1,0:T(8,128)S(1)} %get-tuple-element.743, f32[16,128]{1,0:T(8,128)S(1)} %get-tuple-element.744, f32[256]{0:T(256)S(1)} %fusion.91, ...), kind=kLoop, calls=%fused_computation.35.clone.1 | loop fusion | flops 8910848 | bytes 6382592 | tf_op jit(solution)/shard_map/while/body/reduce_sum | solution.py:106
  163.9 24.5 %scatter_custom_fusion = f32[65,8192]{0,1:T(8,128)} fusion(s32[4096]{0:T(1024)S(1)} %bitcast.103, f32[4096,65]{1,0:T(8,128)S(1)} %bitcast.99, f32[]{:T(128)} %constant.142.clone.1), kind=kCustom, calls=%fused_computation.73 | custom fusion | flops 266240 | bytes 2129924 | tf_op jit(solution)/shard_map/scatter-add | solution.py:161
  190.9 1.9 collective-permute-start.1
  192.9 13.7 %collective-permute-done.1 = f32[65,4096]{1,0:T(8,128)} collective-permute-done((f32[65,4096]{1,0:T(8,128)S(1)}, f32[65,4096]{1,0:T(8,128)}, u32[]{:S(2)}, u32[]{:S(2)}) %collective-permute-start.1) | collective-permute-done | bytes 1064992 | tf_op jit(solution)/shard_map/ppermute | solution.py:12
  206.6 1.8 copy.66
  208.4 3.1 %slice_add_fusion = f32[65,4096]{0,1:T(8,128)} fusion(f32[65,4096]{0,1:T(8,128)S(1)} %copy.66, f32[65,8192]{0,1:T(8,128)} %scatter_custom_fusion), kind=kLoop, calls=%fused_computation.72 | loop fusion | flops 266240 | bytes 3194880 | tf_op jit(solution)/shard_map/add | solution.py:164
  211.5 75.5 %reduce-scatter.2.cloned.1.call-done = f32[65,256]{0,1:T(8,128)} async-done(((f32[65,4096]{0,1:T(8,128)}), f32[65,256]{0,1:T(8,128)}) %reduce-scatter.2.cloned.1.call-update) | async-done | bytes 66576 | tf_op jit(solution)/shard_map/reduce_scatter | solution.py:163
  (96 shorter events, 30.1 us)
Async XLA Ops:
  7.2 122.7 %copy-start = (bf16[64,512]{1,0:T(8,128)(2,1)S(1)}, bf16[64,512]{1,0:T(8,128)(2,1)}, u32[]{:S(2)}) copy-start(bf16[64,512]{1,0:T(8,128)(2,1)} %param.18) | copy-start | bytes 196612
  7.2 87.2 %all-gather.3.cloned.1.call-start = ((), (), s32[]{:S(2)}) async-start(), calls=%async_computation.2 | async-start | bytes 2506752 | tf_op jit(solution)/shard_map/all_gather | solution.py:149
  8.1 12.4 %collective-permute-start = (f32[69,256]{1,0:T(8,128)S(1)}, f32[69,256]{1,0:T(8,128)S(1)}, u32[]{:S(2)}, u32[]{:S(2)}) collective-permute-start(f32[69,256]{1,0:T(8,128)S(1)} %get-tuple-element.528), channel_id=1, source_target_pairs={{0,1},{1,2},{2,3},{3,4},{4,5},{5,6},{6,7},{7,8},{8,9},{9,10},{10,1... | collective-permute-start | bytes 211976 | tf_op jit(solution)/shard_map/ppermute | solution.py:12
  21.2 265.9 %reduce-scatter.2.cloned.1.call-start = ((), (), s32[]{:S(2)}) async-start(), calls=%async_computation.1 | async-start | bytes 2228224 | tf_op jit(solution)/shard_map/reduce_scatter | solution.py:163
  116.9 1.2 copy-start.2
  129.9 2.2 copy-start.1
  188.4 1.6 slice-start
  190.9 15.6 %collective-permute-start.1 = (f32[65,4096]{1,0:T(8,128)S(1)}, f32[65,4096]{1,0:T(8,128)}, u32[]{:S(2)}, u32[]{:S(2)}) collective-permute-start(f32[65,4096]{1,0:T(8,128)S(1)} %copy.65), channel_id=1, source_target_pairs={{1,0},{2,1},{3,2},{4,3},{5,4},{6,5},{7,6},{8,7},{9,8},{10,9},{11,1... | collective-permute-start | bytes 3194888 | tf_op jit(solution)/shard_map/ppermute | solution.py:12
Sparse Core Ops, SparseCore 0:
  21.3 73.0 all-gather.2
  211.6 75.3 reduce-scatter.1
